TPU v7x, 256 devices: a whole 4x4x8 slice. The times are simulated.
256 devices in a mesh: dom: 8 (over x, core), mem: 32 (over z, y).
Axes of the slice: x: 4, y: 4, z: 8, core: 2. Of those that a mesh axis runs over, the one named last changes fastest.
Arguments:
- state: float32 [1024, 262144], P('mem', 'dom'), may hold values from -14 to 14, as said below
- obs_ensemble: float32 [1024, 4096], P('mem', 'dom'), may hold values from -14 to 14, as said below
- innovations: float32 [1024, 4096], P('mem', 'dom'), may hold values from -6 to 6
- obs_coords: float32 [2, 4096], P(None, 'dom'), may hold values from 0 to 8, as said below
- tile_list: int32 [8, 32, 2, 48], P('dom', 'mem'), may hold values from 0 to 11, as said below
- tile_counts: int32 [8, 32], P('dom', 'mem'), may hold values from 24 to 48, as said below
Outputs:
- analysis: float32 [1024, 262144], P(None, ('dom', 'mem'))
Inputs may be any that keep to these rules, and one draw needn't show every extreme that they name: `state`: forecast values of each gridpoint: an offset plus a spread of its own times a bounded noise. `obs_ensemble`: Observation-space values of each observation: an offset plus a spread of its own times a bounded noise. `obs_coords`: the observations of domain d have a first coordinate within [d, d + 1) and a second within [0, 1). `tile_list`: slots k * 6 to (k + 1) * 6 - 1 name point block k (of 8) and 6 distinct observation blocks of the window of 12 blocks: the left neighbour domain's, the own domain's, the right neighbour domain's, domains on a cycle. `tile_counts`: slots below the count are live. Some group has all 48 live, some other group half of them.
All inputs are finite; a program needn't handle non-finite values.
Results may differ from a plain program's by a relative error of at most 0.0002.
Values sent between devices are 32-bit elements; how exact they have to be, the bound alone decides.
A program may use at most 192 MiB of HBM per device.

v0:
```python
import jax
import jax.numpy as jnp
from jax import lax
from jax.sharding import PartitionSpec as P

taper_reach = 0.6
highest = lax.Precision.HIGHEST


def side_by_side(arrays, axis, dim, along):
    widths = [a.shape[along] for a in arrays]
    both = jnp.concatenate(arrays, axis=along)
    out = lax.all_gather(both, axis, axis=dim, tiled=True)
    return tuple(jnp.split(out, [sum(widths[:k]) for k in range(1, len(widths))], axis=along))


def padded(block, sides, width):
    for axis, dim in sides:
        count = lax.axis_size(axis)
        forward = [(i, i + 1) for i in range(count - 1)]
        forward.append((count - 1, 0))
        backward = [(target, source) for source, target in forward]
        low = lax.ppermute(
            lax.slice_in_dim(block, block.shape[dim] - width, None, axis=dim), axis, forward
        )
        high = lax.ppermute(lax.slice_in_dim(block, 0, width, axis=dim), axis, backward)
        block = jnp.concatenate([low, block, high], axis=dim)
    return block


def split_up(x, dim, count):
    before, after = (x.shape[:dim], x.shape[dim + 1 :])
    return jnp.moveaxis(x.reshape(*before, count, -1, *after), dim, 0)


def piece_ends(length, count):
    unit = 8 if length >= 8 * count else 1
    return [length // unit * k // count * unit for k in range(1, count)]


def laid_out(tiles, dim):
    tiles = jnp.moveaxis(tiles, 0, dim)
    shape = tiles.shape
    return tiles.reshape(*shape[:dim], shape[dim] * shape[dim + 1], *shape[dim + 2 :])


def exchange_in_pieces(x, axis, pieces, split_dim, concat_dim):
    tiles = split_up(x, split_dim, lax.axis_size(axis))
    cut = max(range(1, max(2, tiles.ndim - 1)), key=lambda d: tiles.shape[d])
    finished = []
    for share in jnp.split(tiles, piece_ends(tiles.shape[cut], pieces), axis=cut):
        if share.size:
            finished.append(lax.all_to_all(share, axis, split_axis=0, concat_axis=0, tiled=True))
    return laid_out(jnp.concatenate(finished, axis=cut), concat_dim)


def taper_of(point_x, point_y, obs_x, obs_y, cycle_size):
    gap_x = jnp.abs(point_x[:, :, None] - obs_x[:, None, :])
    gap_x = jnp.minimum(gap_x, cycle_size - gap_x)
    gap_y = point_y[:, :, None] - obs_y[:, None, :]
    return jnp.exp(-(gap_x * gap_x + gap_y * gap_y) / (2.0 * taper_reach * taper_reach))


def shards(state, obs_ensemble, innovations, obs_coords, tile_list, tile_counts):
    members_local = state.shape[0]
    groups = lax.axis_size("mem")
    per_domain = state.shape[1]
    per_device = per_domain // groups
    obs_local = obs_ensemble.shape[1]
    members = members_local * groups
    full_ens, full_innov = side_by_side((obs_ensemble, innovations), "mem", 0, 1)
    anomalies = full_ens - jnp.mean(full_ens, axis=0, keepdims=True)
    stacked = jnp.concatenate([anomalies, full_innov, obs_coords], axis=0)
    window = padded(stacked, (("dom", 1),), obs_local)
    anom_win = window[:members]
    innov_win = window[members : 2 * members]
    coord_win = window[2 * members :]
    states = exchange_in_pieces(state, "mem", 2, 1, 0)
    tile_side = 128
    nblocks = per_device // tile_side
    wblocks = 3 * obs_local // tile_side
    point_grid = states.reshape(members, nblocks, tile_side)
    anom_grid = anom_win.reshape(members, wblocks, tile_side)
    innov_grid = innov_win.reshape(members, wblocks, tile_side)
    obs_x = coord_win[0].reshape(wblocks, tile_side)
    obs_y = coord_win[1].reshape(wblocks, tile_side)
    domain = lax.axis_index("dom")
    start_index = lax.axis_index("mem") * per_device
    within = start_index + jnp.arange(per_device, dtype=jnp.int32)
    pts_x = (domain.astype(jnp.float32) + ((within % 32).astype(jnp.float32) + 0.5) / 32.0).reshape(
        nblocks, tile_side
    )
    pts_y = (((within // 32).astype(jnp.float32) + 0.5) / float(per_domain // 32)).reshape(
        nblocks, tile_side
    )
    cycle_size = float(lax.axis_size("dom"))
    pblocks = tile_list[0, 0, 0]
    oblocks = tile_list[0, 0, 1]
    tiles_total = pblocks.shape[0]
    live_mask = (jnp.arange(tiles_total, dtype=jnp.int32) < tile_counts[0, 0]).astype(jnp.float32)
    batch_size = min(tiles_total, 24)
    batches = tiles_total // batch_size
    block_ids = jnp.arange(nblocks, dtype=jnp.int32)

    def tile_batch(change, batch):
        point_ids, obs_ids, alive = batch
        x_blocks = jnp.take(point_grid, point_ids, axis=1)
        y_blocks = jnp.take(anom_grid, obs_ids, axis=1)
        w_blocks = jnp.take(innov_grid, obs_ids, axis=1)
        covariance = jnp.einsum("mti,mtj->tij", x_blocks, y_blocks, precision=highest) / (
            members - 1
        )
        taper = taper_of(
            jnp.take(pts_x, point_ids, axis=0),
            jnp.take(pts_y, point_ids, axis=0),
            jnp.take(obs_x, obs_ids, axis=0),
            jnp.take(obs_y, obs_ids, axis=0),
            cycle_size,
        )
        weights = taper * covariance * alive[:, None, None]
        increment = jnp.einsum("mtj,tij->mti", w_blocks, weights, precision=highest)
        onehot = (point_ids[:, None] == block_ids[None, :]).astype(jnp.float32)
        change = change + jnp.einsum("mti,tp->mpi", increment, onehot, precision=highest)
        return (change, None)

    change, _ = lax.scan(
        tile_batch,
        jnp.zeros((members, nblocks, tile_side), jnp.float32),
        (
            pblocks.reshape(batches, batch_size),
            oblocks.reshape(batches, batch_size),
            live_mask.reshape(batches, batch_size),
        ),
    )
    return states + change.reshape(members, per_device)


def solution(mesh):
    return jax.shard_map(
        shards,
        mesh=mesh,
        in_specs=(
            P("mem", "dom"),
            P("mem", "dom"),
            P("mem", "dom"),
            P(None, "dom"),
            P("dom", "mem", None, None),
            P("dom", "mem"),
        ),
        out_specs=P(None, ("dom", "mem")),
        check_vma=False,
    )
```

profile of v0, /device:TPU:2, one launch (start us, length us, event | category | flops | bytes accessed | tf_op | source)
XLA Modules:
  0.0 420.7 jit_solution(9619973472683127624)
XLA Ops:
  13.0 11.7 %all-to-all-start = ((f32[32,16,1024]{2,1,0:T(8,128)}), f32[32,16,1024]{2,1,0:T(8,128)}, u32[]{:S(2)}, u32[]{:S(2)}) async-start(f32[32,16,1024]{2,1,0:T(8,128)} %get-tuple-element.265), calls=%async_computation | async-start | bytes 4194304 | tf_op jit(solution)/shard_map/all_to_all | solution.py:53
  24.9 78.7 %all-gather.2.cloned.1.call-done = f32[1024,1024]{1,0:T(8,128)} async-done(((f32[32,1024]{1,0:T(8,128)}), f32[1024,1024]{1,0:T(8,128)}) %all-gather.2.cloned.1.call-update) | async-done | bytes 4194320 | tf_op jit(solution)/shard_map/all_gather | solution.py:13
  103.6 4.1 slice_reduce_fusion.2
  111.5 3.2 broadcast_subtract_fusion
  114.7 7.5 %all-to-all-start.1 = ((f32[32,16,1024]{2,1,0:T(8,128)}), f32[32,16,1024]{2,1,0:T(8,128)}, u32[]{:S(2)}, u32[]{:S(2)}) async-start(f32[32,16,1024]{2,1,0:T(8,128)} %get-tuple-element.264), calls=%async_computation.1 | async-start | bytes 4194304 | tf_op jit(solution)/shard_map/all_to_all | solution.py:53
  122.1 4.0 pad_maximum_fusion.5
  126.1 5.8 %copy.29 = f32[2050,512]{1,0:T(8,128)} copy(f32[2050,512]{0,1:T(8,128)} %pad_maximum_fusion.5) | data formatting | bytes 8396800 | tf_op jit(solution)/shard_map/concatenate | solution.py:73
  134.5 3.2 constant_dynamic-update-slice_fusion.1
  137.7 30.8 %all-to-all-done.1 = f32[32,16,1024]{2,1,0:T(8,128)} async-done(((f32[32,16,1024]{2,1,0:T(8,128)}), f32[32,16,1024]{2,1,0:T(8,128)}, u32[]{:S(2)}, u32[]{:S(2)}) %all-to-all-start.1) | async-done | bytes 2097184 | tf_op jit(solution)/shard_map/all_to_all | solution.py:53
  168.5 3.2 constant_dynamic-update-slice_fusion
  171.6 3.2 copy.41
  180.3 5.5 %copy.31 = f32[2050,512]{0,1:T(8,128)} copy(f32[2050,512]{1,0:T(8,128)} %collective-permute-done) | data formatting | bytes 8396800 | tf_op jit(solution)/shard_map/ppermute | solution.py:23
  185.8 5.6 %copy.32 = f32[2050,512]{0,1:T(8,128)} copy(f32[2050,512]{1,0:T(8,128)} %collective-permute-done.1) | data formatting | bytes 8396800 | tf_op jit(solution)/shard_map/ppermute | solution.py:26
  191.3 8.7 %pad_maximum_fusion = (f32[1024,1536]{0,1:T(8,128)}, f32[1024,1536]{0,1:T(8,128)}) fusion(f32[2050,512]{0,1:T(8,128)} %copy.32, f32[2050,512]{0,1:T(8,128)} %copy.31, f32[2,512]{0,1:T(8,128)S(1)} %copy.28, f32[1024,512]{0,1:T(8,128)S(1)} %copy.38, f32[1024,512]{0,1:T(8,128)} %broadcast_subtract_fusion), kind=kLoop, calls=%fused_computation.90 | loop fusion | flops 12582912 | bytes 25178112 | tf_op jit(solution)/shard_map/concatenate | solution.py:27
  201.8 6.6 %copy.34 = f32[1024,12,128]{2,0,1:T(8,128)} copy(f32[1024,12,128]{0,2,1:T(8,128)} %bitcast.81) | data formatting | bytes 12582912
  208.5 6.6 %copy.35 = f32[1024,12,128]{2,0,1:T(8,128)} copy(f32[1024,12,128]{0,2,1:T(8,128)} %bitcast.80) | data formatting | bytes 12582912
  215.1 191.7 %while.13 = (s32[]{:T(128)}, f32[1024,8,128]{2,1,0:T(8,128)}, s32[2,24]{1,0:T(2,128)S(1)}, s32[2,24]{1,0:T(2,128)S(1)}, f32[12,128]{1,0:T(8,128)S(1)}, /*index=5...) while((s32[]{:T(128)}, f32[1024,8,128]{2,1,0:T(8,128)}, ...), condition=%wide.region_2.6_spmd.clone.clone.clone, body=%wide.region_1.5_spmd.clone.clone.clone.sunk | while | flops 9982357504 | bytes 175380896 | solution.py:126
  215.1 9.8 %gather_fusion.1 = f32[24,1024,128]{2,1,0:T(8,128)} fusion(f32[1024,12,128]{2,0,1:T(8,128)} %get-tuple-element.399, s32[1024]{0:T(1024)S(1)} %pad_clamp_fusion.6), kind=kCustom, calls=%fused_computation.2.clone.clone.1 | custom fusion | bytes 25165920 | tf_op jit(solution)/shard_map/while/body/eval_jaxpr/jit(_take)/gather | solution.py:108
  225.0 9.3 %gather_fusion.2 = f32[24,1024,128]{2,1,0:T(8,128)} fusion(f32[1024,8,128]{2,0,1:T(8,128)} %get-tuple-element.398, s32[1024]{0:T(1024)S(1)} %pad_clamp_fusion.7), kind=kCustom, calls=%fused_computation.6.clone.clone.clone.clone.1 | custom fusion | bytes 25165920 | tf_op jit(solution)/shard_map/while/body/eval_jaxpr/jit(_take)/gather | solution.py:107
  234.3 25.6 %fusion.86 = f32[24,128,128]{2,1,0:T(8,128)S(1)} fusion(f32[24,1024,128]{2,1,0:T(8,128)} %gather_fusion.1, f32[24,1024,128]{2,1,0:T(8,128)} %gather_fusion.2, pred[24]{0:T(512)(128)(4,1)S(1)} %get-tuple-element.355, pred[24]{0:T(512)(128)(4,1)S(1)} %get-tuple-element.356), kind=kOutput, calls=%fused_computation.12.clone.1 | convolution fusion | flops 4838129664 | bytes 26738736 | tf_op jit(solution)/shard_map/while/body/eval_jaxpr/mti,mtj->tij/dot_general | solution.py:110
  262.4 9.8 %gather_fusion = f32[24,1024,128]{2,1,0:T(8,128)} fusion(f32[1024,12,128]{2,0,1:T(8,128)} %get-tuple-element.401, s32[1024]{0:T(1024)S(1)} %pad_clamp_fusion.6), kind=kCustom, calls=%fused_computation.5.clone.clone.1 | custom fusion | bytes 25165920 | tf_op jit(solution)/shard_map/while/body/eval_jaxpr/jit(_take)/gather | solution.py:109
  272.2 17.0 %fusion.89 = f32[1024,24,128]{0,2,1:T(8,128)} fusion(f32[24,1024,128]{2,1,0:T(8,128)} %gather_fusion, pred[24]{0:T(512)(128)(4,1)S(1)} %get-tuple-element.355, f32[24,128,128]{2,1,0:T(8,128)S(1)} %fusion.86, f32[24]{0:T(128)S(1)} %fusion.87, f32[24,128]{1,0:T(8,128)S(1)} %get-tuple-element.357, f32[24,128]{1,0:T(8,128)S(1)} %get-tuple-element.361, ...), kind=kOutput, calls=%fused_computation.23.clone.1 | convolution fusion | flops 4840095744 | bytes 26787960 | tf_op jit(solution)/shard_map/while/body/eval_jaxpr/mtj,tij->mti/dot_general | solution.py:121
  289.3 12.6 %copy.47 = f32[1024,24,128]{2,1,0:T(8,128)} copy(f32[1024,24,128]{0,2,1:T(8,128)} %fusion.89) | data formatting | bytes 25165824 | tf_op jit(solution)/shard_map/while/body/eval_jaxpr/mtj,tij->mti/transpose | solution.py:121
  301.9 8.8 %bitcast_add_fusion.3 = f32[1024,8,128]{2,1,0:T(8,128)} fusion(f32[1024,8,128]{2,1,0:T(8,128)} %get-tuple-element.379, f32[1024,24,128]{2,1,0:T(8,128)} %copy.47, pred[]{:T(512)S(6)} %compare.10, s32[24]{0:T(128)S(1)} %get-tuple-element.353), kind=kOutput, calls=%fused_computation.24.clone.1 | convolution fusion | flops 304087232 | bytes 20971616 | tf_op jit(solution)/shard_map/while/body/eval_jaxpr/mti,tp->mpi/dot_general | solution.py:123
  310.7 9.8 %gather_fusion.1 = f32[24,1024,128]{2,1,0:T(8,128)} fusion(f32[1024,12,128]{2,0,1:T(8,128)} %get-tuple-element.399, s32[1024]{0:T(1024)S(1)} %pad_clamp_fusion.6), kind=kCustom, calls=%fused_computation.2.clone.clone.1 | custom fusion | bytes 25165920 | tf_op jit(solution)/shard_map/while/body/eval_jaxpr/jit(_take)/gather | solution.py:108
  320.5 9.3 %gather_fusion.2 = f32[24,1024,128]{2,1,0:T(8,128)} fusion(f32[1024,8,128]{2,0,1:T(8,128)} %get-tuple-element.398, s32[1024]{0:T(1024)S(1)} %pad_clamp_fusion.7), kind=kCustom, calls=%fused_computation.6.clone.clone.clone.clone.1 | custom fusion | bytes 25165920 | tf_op jit(solution)/shard_map/while/body/eval_jaxpr/jit(_take)/gather | solution.py:107
  329.8 25.6 %fusion.86 = f32[24,128,128]{2,1,0:T(8,128)S(1)} fusion(f32[24,1024,128]{2,1,0:T(8,128)} %gather_fusion.1, f32[24,1024,128]{2,1,0:T(8,128)} %gather_fusion.2, pred[24]{0:T(512)(128)(4,1)S(1)} %get-tuple-element.355, pred[24]{0:T(512)(128)(4,1)S(1)} %get-tuple-element.356), kind=kOutput, calls=%fused_computation.12.clone.1 | convolution fusion | flops 4838129664 | bytes 26738736 | tf_op jit(solution)/shard_map/while/body/eval_jaxpr/mti,mtj->tij/dot_general | solution.py:110
  357.9 9.8 %gather_fusion = f32[24,1024,128]{2,1,0:T(8,128)} fusion(f32[1024,12,128]{2,0,1:T(8,128)} %get-tuple-element.401, s32[1024]{0:T(1024)S(1)} %pad_clamp_fusion.6), kind=kCustom, calls=%fused_computation.5.clone.clone.1 | custom fusion | bytes 25165920 | tf_op jit(solution)/shard_map/while/body/eval_jaxpr/jit(_take)/gather | solution.py:109
  367.8 17.0 %fusion.89 = f32[1024,24,128]{0,2,1:T(8,128)} fusion(f32[24,1024,128]{2,1,0:T(8,128)} %gather_fusion, pred[24]{0:T(512)(128)(4,1)S(1)} %get-tuple-element.355, f32[24,128,128]{2,1,0:T(8,128)S(1)} %fusion.86, f32[24]{0:T(128)S(1)} %fusion.87, f32[24,128]{1,0:T(8,128)S(1)} %get-tuple-element.357, f32[24,128]{1,0:T(8,128)S(1)} %get-tuple-element.361, ...), kind=kOutput, calls=%fused_computation.23.clone.1 | convolution fusion | flops 4840095744 | bytes 26787960 | tf_op jit(solution)/shard_map/while/body/eval_jaxpr/mtj,tij->mti/dot_general | solution.py:121
  384.8 12.6 %copy.47 = f32[1024,24,128]{2,1,0:T(8,128)} copy(f32[1024,24,128]{0,2,1:T(8,128)} %fusion.89) | data formatting | bytes 25165824 | tf_op jit(solution)/shard_map/while/body/eval_jaxpr/mtj,tij->mti/transpose | solution.py:121
  397.4 9.4 %bitcast_add_fusion.3 = f32[1024,8,128]{2,1,0:T(8,128)} fusion(f32[1024,8,128]{2,1,0:T(8,128)} %get-tuple-element.379, f32[1024,24,128]{2,1,0:T(8,128)} %copy.47, pred[]{:T(512)S(6)} %compare.10, s32[24]{0:T(128)S(1)} %get-tuple-element.353), kind=kOutput, calls=%fused_computation.24.clone.1 | convolution fusion | flops 304087232 | bytes 20971616 | tf_op jit(solution)/shard_map/while/body/eval_jaxpr/mti,tp->mpi/dot_general | solution.py:123
  406.8 7.0 %bitcast_add_fusion.1 = f32[1024,1024]{1,0:T(8,128)} fusion(f32[128,8,8,128]{3,2,1,0:T(8,128)} %bitcast.74, f32[32,32,1024]{2,1,0:T(8,128)} %constant_dynamic-update-slice_fusion), kind=kLoop, calls=%fused_computation.96 | loop fusion | flops 1048576 | bytes 12582912 | tf_op jit(solution)/shard_map/add | solution.py:135
  (58 shorter events, 24.6 us)
Async XLA Ops:
  6.5 97.1 %all-gather.2.cloned.1.call-start = ((), (), s32[]{:S(2)}) async-start(), calls=%async_computation.2 | async-start | bytes 4325376 | tf_op jit(solution)/shard_map/all_gather | solution.py:13
  13.0 11.8 %copy-start = (f32[2,512]{1,0:T(2,128)S(1)}, f32[2,512]{1,0:T(2,128)}, u32[]{:S(2)}) copy-start(f32[2,512]{1,0:T(2,128)} %param.17) | copy-start | bytes 12292
  13.0 101.7 %all-to-all-start = ((f32[32,16,1024]{2,1,0:T(8,128)}), f32[32,16,1024]{2,1,0:T(8,128)}, u32[]{:S(2)}, u32[]{:S(2)}) async-start(f32[32,16,1024]{2,1,0:T(8,128)} %get-tuple-element.265), calls=%async_computation | async-start | bytes 4194304 | tf_op jit(solution)/shard_map/all_to_all | solution.py:53
  114.7 53.8 %all-to-all-start.1 = ((f32[32,16,1024]{2,1,0:T(8,128)}), f32[32,16,1024]{2,1,0:T(8,128)}, u32[]{:S(2)}, u32[]{:S(2)}) async-start(f32[32,16,1024]{2,1,0:T(8,128)} %get-tuple-element.264), calls=%async_computation.1 | async-start | bytes 4194304 | tf_op jit(solution)/shard_map/all_to_all | solution.py:53
  126.1 7.5 %copy-start.1 = (s32[1,1,2,48]{3,2,1,0:T(2,128)S(1)}, s32[1,1,2,48]{3,2,1,0:T(2,128)}, u32[]{:S(2)}) copy-start(s32[1,1,2,48]{3,2,1,0:T(2,128)} %param.18) | copy-start | bytes 1156
  131.9 48.4 %collective-permute-start = (f32[2050,512]{1,0:T(8,128)}, f32[2050,512]{1,0:T(8,128)}, u32[]{:S(2)}, u32[]{:S(2)}) collective-permute-start(f32[2050,512]{1,0:T(8,128)} %copy.29), channel_id=1, source_target_pairs={{0,32},{32,64},{64,96},{96,128},{128,160},{160,192},{192,224},{224... | collective-permute-start | bytes 12595208 | tf_op jit(solution)/shard_map/ppermute | solution.py:23
  131.9 53.9 %collective-permute-start.1 = (f32[2050,512]{1,0:T(8,128)}, f32[2050,512]{1,0:T(8,128)}, u32[]{:S(2)}, u32[]{:S(2)}) collective-permute-start(f32[2050,512]{1,0:T(8,128)} %copy.29), channel_id=1, source_target_pairs={{32,0},{64,32},{96,64},{128,96},{160,128},{192,160},{224,192},{0,2... | collective-permute-start | bytes 12595208 | tf_op jit(solution)/shard_map/ppermute | solution.py:26
  185.8 14.3 %slice-start = ((s8[4456448]{0:T(1024)(128)(4,1)}), s8[262144]{0:T(1024)(128)(4,1)S(1)}, s32[]{:S(2)}) async-start(s8[4456448]{0:T(1024)(128)(4,1)} %bitcast.75), calls=%async_computation.3 | async-start | bytes 524288
  191.3 8.7 %slice-start.1 = ((s8[4456448]{0:T(1024)(128)(4,1)}), s8[4194304]{0:T(1024)(128)(4,1)S(1)}, s32[]{:S(2)}) async-start(s8[4456448]{0:T(1024)(128)(4,1)} %bitcast.75), calls=%async_computation.4 | async-start | bytes 8388608
Sparse Core Ops, SparseCore 0:
  9.9 93.6 all-gather.1
where the time goes:
time: 424 us; the launch traced here: 421 us
  local copies, waits for them, and re-layouts  139 us (33%)
  waiting for transfers between devices  112 us (26%)
  matrix products  104 us (25%)
  other arithmetic  30.7 us (7%)
  starting transfers between devices  21 us (5%)
  between operations  14.1 us (3%)
    all_gather x1, waiting for transfers between devices, side_by_side(): out = lax.all_gather(both, axis, axis=dim, tiled=True)  78.7 us
    dot_general x2, matrix products, tile_batch(): jnp.einsum('mti,mtj->tij', x_blocks, y_blocks, precision=highest)  51.3 us
    dot_general x2, matrix products, tile_batch(): increment = jnp.einsum('mtj,tij->mti', w_blocks, weights, precision=highest)  34.1 us
    all_to_all x2, waiting for transfers between devices, exchange_in_pieces(): lax.all_to_all(share, axis, split_axis=0, concat_axis=0, tiled=True)  30.8 us
    unnamed x16, local copies, waits for them, and re-layouts  26.4 us
    transpose x2, local copies, waits for them, and re-layouts, tile_batch(): increment = jnp.einsum('mtj,tij->mti', w_blocks, weights, precision=highest)  25.2 us
    gather x2, local copies, waits for them, and re-layouts, tile_batch(): y_blocks = jnp.take(anom_grid, obs_ids, axis=1)  19.7 us
    gather x2, local copies, waits for them, and re-layouts, tile_batch(): w_blocks = jnp.take(innov_grid, obs_ids, axis=1)  19.7 us
  transfers between devices with their start and end apart: 5, of which 3 were waited for; matrix products, arithmetic and copies ran while one was open for 10% of the time, Pallas kernels for 0%

commit v1 on v0

v1 whole, which is shorter than its diff:
```python
import jax
import jax.numpy as jnp
from jax import lax
from jax.experimental import pallas as pl
from jax.experimental.pallas import tpu as pltpu
from jax.sharding import PartitionSpec as P

taper_reach = 0.6
f32, bf16 = jnp.float32, jnp.bfloat16
ZN, YN = 8, 4
MEM = ZN * YN
DOM = 8
ROWS = 32
M = 1024
OBS = 512
BLK = 128
NB = 8
TPB = 6
PTS = NB * BLK


def halves(v):
    high = v.astype(bf16)
    return high, (v - high.astype(f32)).astype(bf16)


def remote(src, dst, send, recv, device):
    return pltpu.make_async_remote_copy(
        src_ref=src,
        dst_ref=dst,
        send_sem=send,
        recv_sem=recv,
        device_id=device,
        device_id_type=pl.DeviceIdType.MESH,
    )


def kernel(
    tiles, count, state, ens, innov, coords, out,
    xbuf, win, crd, at_hi, at_lo, in_hi, in_lo, cx, cy, obuf,
    obs_local, own_local, crd_send, z_send, y_send, x_send, a_send,
    blk_recv, x_recv, crd_recv, a_recv, out_sem,
):
    d = lax.axis_index("dom")
    me = lax.axis_index("mem")
    z, y = lax.div(me, YN), lax.rem(me, YN)
    right, left = lax.rem(d + 1, DOM), lax.rem(d + DOM - 1, DOM)

    def mem_of(dz, dy):
        return lax.rem(z + dz + ZN, ZN) * YN + lax.rem(y + dy + YN, YN)

    def rows(m):
        return pl.ds(pl.multiple_of(m * ROWS, ROWS), ROWS)

    own_obs = [
        pltpu.make_async_copy(ens, win.at[1, 0, rows(me), :], obs_local.at[0]),
        pltpu.make_async_copy(innov, win.at[1, 1, rows(me), :], obs_local.at[1]),
        pltpu.make_async_copy(coords, crd.at[1], obs_local.at[2]),
    ]
    for c in own_obs:
        c.start()

    def own_state(k):
        cols = pl.ds(pl.multiple_of(me * PTS + k * BLK, BLK), BLK)
        return pltpu.make_async_copy(state.at[:, cols], xbuf.at[k, rows(me), :], own_local.at[k])

    for k in range(NB):
        own_state(k).start()

    barrier = pltpu.get_barrier_semaphore()

    def greet(i, c):
        pl.semaphore_signal(
            barrier, inc=1, device_id=(d, lax.rem(me + i, MEM)), device_id_type=pl.DeviceIdType.MESH
        )
        return c

    for other in (left, right):
        pl.semaphore_signal(
            barrier, inc=1, device_id=(other, me), device_id_type=pl.DeviceIdType.MESH
        )
    lax.fori_loop(1, MEM, greet, 0)
    pl.semaphore_wait(barrier, MEM + 1)
    for c in own_obs:
        c.wait()

    def block(m):
        return win.at[1, :, rows(m), :]

    def half(t, m):
        return win.at[1, t, rows(m), :]

    def push(src, m, dz, dy, send):
        remote(src, src, send, blk_recv.at[m], (d, mem_of(dz, dy))).start()

    def push_z(m, way):
        push(block(m), m, way, 0, z_send)

    def push_y(m):
        push(block(m), m, 0, 1, y_send)
        push(block(m), m, 0, -1, y_send)

    def push_x(m):
        remote(block(m), win.at[2, :, rows(m), :], x_send.at[0], x_recv.at[1], (left, me)).start()
        remote(block(m), win.at[0, :, rows(m), :], x_send.at[1], x_recv.at[0], (right, me)).start()

    def take(m):
        remote(block(m), block(m), z_send, blk_recv.at[m], (d, mem_of(1, 0))).wait_recv()

    def send_state(k):
        def one(i, c):
            j, dy = lax.rem(i, ZN), lax.div(i, ZN)
            h = lax.div(j + 1, 2)
            dz = jnp.where(lax.rem(j, 2) == 1, h, ZN - h)
            to = mem_of(dz, dy)
            cols = pl.ds(pl.multiple_of(to * PTS + k * BLK, BLK), BLK)
            remote(
                state.at[:, cols], xbuf.at[k, rows(me), :], a_send, a_recv.at[k], (d, to)
            ).start()
            return c

        lax.fori_loop(1, MEM, one, 0)

    def column(dz):
        lo, hi = mem_of(dz, -1), mem_of(dz, 1)
        take(lo)
        push(half(0, lo), lo, 0, 1, y_send)
        push_x(lo)
        take(hi)
        push(half(1, hi), hi, 0, -1, y_send)
        push_x(hi)

    push_z(me, 1)
    push_z(me, -1)
    push_y(me)
    coord_copies = [
        remote(coords, crd.at[2], crd_send.at[0], crd_recv.at[1], (left, me)),
        remote(coords, crd.at[0], crd_send.at[1], crd_recv.at[0], (right, me)),
    ]
    for c in coord_copies:
        c.start()
    push_x(me)
    send_state(0)
    for s in range(1, ZN // 2 + 1):
        if s < ZN // 2:
            up, down = mem_of(-s, 0), mem_of(s, 0)
            for m, way, t in ((up, 1, 0), (down, -1, 1)):
                take(m)
                if s < ZN // 2 - 1:
                    push_z(m, way)
                else:
                    push(half(t, m), m, way, 0, z_send)
                push_y(m)
                push_x(m)
        else:
            m = mem_of(s, 0)
            take(m)
            push_y(m)
            push_x(m)
        column(1 - s)
        if s > 1:
            column(s - 1)
        send_state(s)
    column(ZN // 2)
    send_state(5)

    def far(dz, c):
        m = mem_of(dz, 2)
        take(m)
        push_x(m)
        return c

    lax.fori_loop(0, ZN, far, 0)
    send_state(6)
    send_state(7)

    def prepare(slot):
        def one(j, c):
            b = slot * (OBS // BLK) + j
            cols = pl.ds(pl.multiple_of(j * BLK, BLK), BLK)
            v = win[slot, 0, :, cols]
            v = v - jnp.sum(v, axis=0, keepdims=True) * (1.0 / M)
            at_hi[b], at_lo[b] = halves(v.T)
            in_hi[b], in_lo[b] = halves(win[slot, 1, :, cols])
            cx[b] = jnp.broadcast_to(crd[slot, 0:1, cols], (BLK, BLK)).T
            cy[b] = jnp.broadcast_to(crd[slot, 1:2, cols], (BLK, BLK)).T
            return c

        lax.fori_loop(0, OBS // BLK, one, 0)

    prepare(1)
    for c in coord_copies:
        c.wait()
    for slot, n in ((0, 0), (2, 1)):
        pltpu.make_async_copy(win.at[slot], win.at[slot], x_recv.at[n]).wait()
        prepare(slot)

    def put(k):
        cols = pl.ds(pl.multiple_of(k * BLK, BLK), BLK)
        s = lax.rem(k, 2)
        return pltpu.make_async_copy(obuf.at[s], out.at[:, cols], out_sem.at[s])

    def piece(k, c):
        got = xbuf.at[k, pl.ds(0, M - ROWS), :]
        pltpu.make_async_copy(got, got, a_recv.at[k]).wait()
        own_state(k).wait()
        ids = [tiles[1, k * TPB + t] for t in range(TPB)]
        x = xbuf[k]
        xh, xl = halves(x)
        xs = jnp.concatenate([xh, xl], axis=1)
        ah = jnp.concatenate([at_hi[b] for b in ids], axis=0)
        al = jnp.concatenate([at_lo[b] for b in ids], axis=0)
        c1 = jnp.dot(ah, xs, preferred_element_type=f32)
        c2 = jnp.dot(al, xh, preferred_element_type=f32)
        cov = c1[:, :BLK] + (c1[:, BLK:] + c2)
        lane = lax.broadcasted_iota(jnp.int32, (1, BLK), 1)
        px = d.astype(f32) + (lax.rem(lane, 32).astype(f32) + 0.5) / 32.0
        first = me * (PTS // 32) + k * (BLK // 32)
        py = ((first + lax.div(lane, 32)).astype(f32) + 0.5) / float(MEM * PTS // 32)
        w = []
        for t in range(TPB):
            gx = jnp.abs(px - cx[ids[t]])
            gx = jnp.minimum(gx, float(DOM) - gx)
            gy = py - cy[ids[t]]
            taper = jnp.exp(-(gx * gx + gy * gy) / (2.0 * taper_reach * taper_reach))
            alive = jnp.where(k * TPB + t < count[0, 0], 1.0 / (M - 1), 0.0)
            w.append(taper * cov[t * BLK : (t + 1) * BLK] * alive)
        wh, wl = halves(jnp.concatenate(w, axis=0))
        ws = jnp.concatenate([wh, wl], axis=1)
        ih = jnp.concatenate([in_hi[b] for b in ids], axis=1)
        il = jnp.concatenate([in_lo[b] for b in ids], axis=1)
        r1 = jnp.dot(ih, ws, preferred_element_type=f32)
        r2 = jnp.dot(il, wh, preferred_element_type=f32)

        @pl.when(k >= 2)
        def _():
            put(k - 2).wait()

        obuf[lax.rem(k, 2)] = x + (r1[:, :BLK] + (r1[:, BLK:] + r2))
        put(k).start()
        return c

    lax.fori_loop(0, NB, piece, 0)
    put(NB - 2).wait()
    put(NB - 1).wait()

    def drain(ref, sem):
        pltpu.make_async_copy(ref, ref, sem).wait()

    drain(win.at[1, :, pl.ds(0, 7 * ROWS), :], z_send)
    drain(win.at[1, :, pl.ds(0, 24 * ROWS), :], y_send)
    drain(win.at[1], x_send.at[0])
    drain(win.at[1], x_send.at[1])
    drain(state.at[:, pl.ds(0, (MEM - 1) * PTS)], a_send)


def shards(state, obs_ensemble, innovations, obs_coords, tile_list, tile_counts):
    hbm = pl.BlockSpec(memory_space=pl.ANY)
    smem = pl.BlockSpec(memory_space=pltpu.SMEM)
    vmem = pl.BlockSpec(memory_space=pltpu.VMEM)
    dma = pltpu.SemaphoreType.DMA
    return pl.pallas_call(
        kernel,
        out_shape=jax.ShapeDtypeStruct((M, PTS), f32),
        in_specs=[smem, smem, hbm, hbm, hbm, vmem],
        out_specs=hbm,
        scratch_shapes=[
            pltpu.VMEM((NB, M, BLK), f32),
            pltpu.VMEM((3, 2, M, OBS), f32),
            pltpu.VMEM((3, 2, OBS), f32),
            pltpu.VMEM((12, BLK, M), bf16),
            pltpu.VMEM((12, BLK, M), bf16),
            pltpu.VMEM((12, M, BLK), bf16),
            pltpu.VMEM((12, M, BLK), bf16),
            pltpu.VMEM((12, BLK, BLK), f32),
            pltpu.VMEM((12, BLK, BLK), f32),
            pltpu.VMEM((2, M, BLK), f32),
            dma((3,)),
            dma((NB,)),
            dma((2,)),
            dma,
            dma,
            dma((2,)),
            dma,
            dma((MEM,)),
            dma((2,)),
            dma((2,)),
            dma((NB,)),
            dma((2,)),
        ],
        compiler_params=pltpu.CompilerParams(
            collective_id=0, has_side_effects=True, vmem_limit_bytes=60 * 1024 * 1024
        ),
        name="update",
    )(tile_list[0, 0], tile_counts, state, obs_ensemble, innovations, obs_coords)


def solution(mesh):
    return jax.shard_map(
        shards,
        mesh=mesh,
        in_specs=(
            P("mem", "dom"),
            P("mem", "dom"),
            P("mem", "dom"),
            P(None, "dom"),
            P("dom", "mem", None, None),
            P("dom", "mem"),
        ),
        out_specs=P(None, ("dom", "mem")),
        check_vma=False,
    )
```

time: 424 us -> 121 us (0.29)
  local copies, waits for them, and re-layouts: 139 us -> 4.79 us
  Pallas kernels: 0 us -> 116 us
  waiting for transfers between devices: 112 us -> 0 us
  matrix products: 104 us -> 0 us
  other arithmetic: 30.7 us -> 0 us
  starting transfers between devices: 21 us -> 0 us
  between operations: 14.1 us -> 0.66 us
    pallas_call x0 -> x1, Pallas kernels: none -> 116 us  [shards(): pl.pallas_call(kernel, out_shape=jax.ShapeDtypeStruct((M, PTS), f32), in_...]
    dot_general x6 -> x0, matrix products: 104 us -> none  [the longest x2 51.3 us: tile_batch(): jnp.einsum('mti,mtj->tij', x_blocks, y_blocks, precision=highest)]
    all_gather x1 -> x0, waiting for transfers between devices: 78.7 us -> none  [side_by_side(): out = lax.all_gather(both, axis, axis=dim, tiled=True)]
    gather x14 -> x0, local copies, waits for them, and re-layouts: 62.4 us -> none  [the longest x2 19.7 us: tile_batch(): y_blocks = jnp.take(anom_grid, obs_ids, axis=1)]
    all_to_all x2 -> x0, waiting for transfers between devices: 30.8 us -> none  [exchange_in_pieces(): lax.all_to_all(share, axis, split_axis=0, concat_axis=0, tiled=True)]
    transpose x2 -> x0, local copies, waits for them, and re-layouts: 25.2 us -> none  [tile_batch(): increment = jnp.einsum('mtj,tij->mti', w_blocks, weights, precision=highest)]
    unnamed x16 -> x1, local copies, waits for them, and re-layouts: 26.4 us -> 4.79 us
    all_to_all x2 -> x0, starting transfers between devices: 19.2 us -> none  [exchange_in_pieces(): lax.all_to_all(share, axis, split_axis=0, concat_axis=0, tiled=True)]
  transfers between devices with their start and end apart: 5 -> 0, of which waited for: 3 -> 0; matrix products, arithmetic and copies ran while one was open for 10% -> 0% of each run, Pallas kernels for 0% -> 0%
where the time goes in v1:
time: 121 us
  Pallas kernels  116 us (96%)
  local copies, waits for them, and re-layouts  4.79 us (4%)
    pallas_call x1, Pallas kernels, shards(): pl.pallas_call(kernel, out_shape=jax.ShapeDtypeStruct((M, PTS), f32), in_...  116 us
    unnamed x1, local copies, waits for them, and re-layouts  4.79 us

profile of v1, /device:TPU:2, one launch (start us, length us, event | category | flops | bytes accessed | tf_op | source)
XLA Modules:
  0.0 121.0 jit_solution(13941437720076912169)
XLA Ops:
  0.7 115.6 %update.1 = f32[1024,1024]{1,0:T(8,128)} custom-call(s32[2,48]{1,0:T(2,128)} %bitcast.1, s32[1,1]{1,0:T(1,128)S(6)} %copy.8.count, f32[32,32768]{1,0:T(8,128)} %state.1, f32[32,512]{1,0:T(8,128)} %ens.1, f32[32,512]{1,0:T(8,128)} %innov.1, f32[2,512]{1,0:T(2,128)} %coords.1), custom_call_target="tpu_custom_call" | custom-call | tf_op jit(solution)/shard_map/update/pallas_call | solution.py:262
  116.3 4.8 %copy.9 = f32[1024,1024]{1,0:T(8,128)} copy(f32[1024,1024]{1,0:T(8,128)} %update.1) | data formatting | bytes 8388608

commit v2 on v1

--- a/solution.py
+++ b/solution.py
@@ -36,10 +36,10 @@
 
 
 def kernel(
-    tiles, count, state, ens, innov, coords, out,
-    xbuf, win, crd, at_hi, at_lo, in_hi, in_lo, cx, cy, obuf,
+    tiles_hbm, count, state, ens, innov, coords, out,
+    tiles, xbuf, win, crd, at_hi, at_lo, in_hi, in_lo, cx, cy,
     obs_local, own_local, crd_send, z_send, y_send, x_send, a_send,
-    blk_recv, x_recv, crd_recv, a_recv, out_sem,
+    blk_recv, x_recv, crd_recv, a_recv, token,
 ):
     d = lax.axis_index("dom")
     me = lax.axis_index("mem")
@@ -55,34 +55,29 @@
     own_obs = [
         pltpu.make_async_copy(ens, win.at[1, 0, rows(me), :], obs_local.at[0]),
         pltpu.make_async_copy(innov, win.at[1, 1, rows(me), :], obs_local.at[1]),
+    ]
+    small = [
         pltpu.make_async_copy(coords, crd.at[1], obs_local.at[2]),
+        pltpu.make_async_copy(tiles_hbm, tiles, obs_local.at[3]),
     ]
-    for c in own_obs:
+    for c in own_obs + small:
         c.start()
 
     def own_state(k):
         cols = pl.ds(pl.multiple_of(me * PTS + k * BLK, BLK), BLK)
         return pltpu.make_async_copy(state.at[:, cols], xbuf.at[k, rows(me), :], own_local.at[k])
 
-    for k in range(NB):
-        own_state(k).start()
-
     barrier = pltpu.get_barrier_semaphore()
-
-    def greet(i, c):
-        pl.semaphore_signal(
-            barrier, inc=1, device_id=(d, lax.rem(me + i, MEM)), device_id_type=pl.DeviceIdType.MESH
-        )
-        return c
-
-    for other in (left, right):
-        pl.semaphore_signal(
-            barrier, inc=1, device_id=(other, me), device_id_type=pl.DeviceIdType.MESH
-        )
-    lax.fori_loop(1, MEM, greet, 0)
-    pl.semaphore_wait(barrier, MEM + 1)
+    around = [(d, mem_of(1, 0)), (d, mem_of(-1, 0)), (d, mem_of(0, 1)), (d, mem_of(0, -1))]
+
+    def signal(sem, device):
+        pl.semaphore_signal(sem, inc=1, device_id=device, device_id_type=pl.DeviceIdType.MESH)
+
+    for device in around + [(left, me), (right, me)]:
+        signal(barrier, device)
     for c in own_obs:
         c.wait()
+    pl.semaphore_wait(barrier, 6)
 
     def block(m):
         return win.at[1, :, rows(m), :]
@@ -107,19 +102,26 @@
     def take(m):
         remote(block(m), block(m), z_send, blk_recv.at[m], (d, mem_of(1, 0))).wait_recv()
 
+    def send_to(k, to):
+        cols = pl.ds(pl.multiple_of(to * PTS + k * BLK, BLK), BLK)
+        remote(state.at[:, cols], xbuf.at[k, rows(me), :], a_send, a_recv.at[k], (d, to)).start()
+
+    def send_near(k, c):
+        for dz, dy in ((1, 0), (-1, 0), (0, 1), (0, -1)):
+            send_to(k, mem_of(dz, dy))
+        return c
+
     def send_state(k):
         def one(i, c):
-            j, dy = lax.rem(i, ZN), lax.div(i, ZN)
+            wide, mid = i < ZN, i < 3 * ZN - 2
+            j = jnp.where(wide, i, jnp.where(mid, lax.div(i - ZN, 2), i - (3 * ZN - 2)))
+            dy = jnp.where(wide, 2, jnp.where(mid, 1 + 2 * lax.rem(i, 2), 0))
             h = lax.div(j + 1, 2)
-            dz = jnp.where(lax.rem(j, 2) == 1, h, ZN - h)
-            to = mem_of(dz, dy)
-            cols = pl.ds(pl.multiple_of(to * PTS + k * BLK, BLK), BLK)
-            remote(
-                state.at[:, cols], xbuf.at[k, rows(me), :], a_send, a_recv.at[k], (d, to)
-            ).start()
+            dz = jnp.where(lax.rem(j, 2) == 1, ZN // 2 - h, ZN // 2 + h)
+            send_to(k, mem_of(dz, dy))
             return c
 
-        lax.fori_loop(1, MEM, one, 0)
+        lax.fori_loop(0, MEM - 5, one, 0)
 
     def column(dz):
         lo, hi = mem_of(dz, -1), mem_of(dz, 1)
@@ -139,7 +141,16 @@
     ]
     for c in coord_copies:
         c.start()
+    lax.fori_loop(0, NB - 1, send_near, 0)
     push_x(me)
+    for k in range(NB):
+        own_state(k).start()
+    for n in range(5):
+        side = around[:2] if n < 3 else around[2:]
+        for w in range(2):
+            signal(token.at[n, w], side[w])
+        for w in range(2):
+            pl.semaphore_wait(token.at[n, w], 1)
     send_state(0)
     for s in range(1, ZN // 2 + 1):
         if s < ZN // 2:
@@ -173,6 +184,7 @@
     lax.fori_loop(0, ZN, far, 0)
     send_state(6)
     send_state(7)
+    send_near(NB - 1, 0)
 
     def prepare(slot):
         def one(j, c):
@@ -188,17 +200,14 @@
 
         lax.fori_loop(0, OBS // BLK, one, 0)
 
+    for c in small:
+        c.wait()
     prepare(1)
     for c in coord_copies:
         c.wait()
     for slot, n in ((0, 0), (2, 1)):
         pltpu.make_async_copy(win.at[slot], win.at[slot], x_recv.at[n]).wait()
         prepare(slot)
-
-    def put(k):
-        cols = pl.ds(pl.multiple_of(k * BLK, BLK), BLK)
-        s = lax.rem(k, 2)
-        return pltpu.make_async_copy(obuf.at[s], out.at[:, cols], out_sem.at[s])
 
     def piece(k, c):
         got = xbuf.at[k, pl.ds(0, M - ROWS), :]
@@ -232,17 +241,11 @@
         r1 = jnp.dot(ih, ws, preferred_element_type=f32)
         r2 = jnp.dot(il, wh, preferred_element_type=f32)
 
-        @pl.when(k >= 2)
-        def _():
-            put(k - 2).wait()
-
-        obuf[lax.rem(k, 2)] = x + (r1[:, :BLK] + (r1[:, BLK:] + r2))
-        put(k).start()
+        cols = pl.ds(pl.multiple_of(k * BLK, BLK), BLK)
+        out[:, cols] = x + (r1[:, :BLK] + (r1[:, BLK:] + r2))
         return c
 
     lax.fori_loop(0, NB, piece, 0)
-    put(NB - 2).wait()
-    put(NB - 1).wait()
 
     def drain(ref, sem):
         pltpu.make_async_copy(ref, ref, sem).wait()
@@ -254,17 +257,21 @@
     drain(state.at[:, pl.ds(0, (MEM - 1) * PTS)], a_send)
 
 
+def pinned(a):
+    return a if a.size == 1 else pltpu.with_memory_space_constraint(a, pltpu.HBM)
+
+
 def shards(state, obs_ensemble, innovations, obs_coords, tile_list, tile_counts):
-    hbm = pl.BlockSpec(memory_space=pl.ANY)
-    smem = pl.BlockSpec(memory_space=pltpu.SMEM)
+    hbm = pl.BlockSpec(memory_space=pltpu.HBM)
     vmem = pl.BlockSpec(memory_space=pltpu.VMEM)
     dma = pltpu.SemaphoreType.DMA
     return pl.pallas_call(
         kernel,
-        out_shape=jax.ShapeDtypeStruct((M, PTS), f32),
-        in_specs=[smem, smem, hbm, hbm, hbm, vmem],
-        out_specs=hbm,
+        out_shape=pltpu.VMEM((M, PTS), f32),
+        in_specs=[hbm, pl.BlockSpec(memory_space=pltpu.SMEM), hbm, hbm, hbm, hbm],
+        out_specs=vmem,
         scratch_shapes=[
+            pltpu.SMEM((2, TPB * NB), jnp.int32),
             pltpu.VMEM((NB, M, BLK), f32),
             pltpu.VMEM((3, 2, M, OBS), f32),
             pltpu.VMEM((3, 2, OBS), f32),
@@ -274,8 +281,7 @@
             pltpu.VMEM((12, M, BLK), bf16),
             pltpu.VMEM((12, BLK, BLK), f32),
             pltpu.VMEM((12, BLK, BLK), f32),
-            pltpu.VMEM((2, M, BLK), f32),
-            dma((3,)),
+            dma((4,)),
             dma((NB,)),
             dma((2,)),
             dma,
@@ -286,13 +292,13 @@
             dma((2,)),
             dma((2,)),
             dma((NB,)),
-            dma((2,)),
+            pltpu.SemaphoreType.REGULAR((5, 2)),
         ],
         compiler_params=pltpu.CompilerParams(
-            collective_id=0, has_side_effects=True, vmem_limit_bytes=60 * 1024 * 1024
+            collective_id=0, has_side_effects=True, vmem_limit_bytes=48 * 1024 * 1024
         ),
         name="update",
-    )(tile_list[0, 0], tile_counts, state, obs_ensemble, innovations, obs_coords)
+    )(*(pinned(a) for a in (tile_list[0, 0], tile_counts, state, obs_ensemble, innovations, obs_coords)))
 
 
 def solution(mesh):

time: 121 us -> 116 us (0.959)
  Pallas kernels: 116 us -> 113 us
  local copies, waits for them, and re-layouts: 4.79 us -> 2.02 us
    unnamed x1, local copies, waits for them, and re-layouts: 4.79 us -> 2.02 us
    pallas_call x1, Pallas kernels: 116 us -> 113 us  [shards(): pl.pallas_call(kernel, out_shape=pltpu.VMEM((M, PTS), f32), in_specs=[hbm...]
where the time goes in v2:
time: 116 us
  Pallas kernels  113 us (97%)
  local copies, waits for them, and re-layouts  2.02 us (2%)
    pallas_call x1, Pallas kernels, shards(): pl.pallas_call(kernel, out_shape=pltpu.VMEM((M, PTS), f32), in_specs=[hbm...  113 us

profile of v2, /device:TPU:2, one launch (start us, length us, event | category | flops | bytes accessed | tf_op | source)
XLA Modules:
  0.0 115.7 jit_solution(10457079556927819659)
XLA Ops:
  0.7 113.0 %update.1 = f32[1024,1024]{1,0:T(8,128)S(1)} custom-call(s32[2,48]{1,0:T(2,128)} %bitcast.1, s32[1,1]{1,0:T(1,128)S(6)} %copy.9.count, f32[32,32768]{1,0:T(8,128)} %state.1, f32[32,512]{1,0:T(8,128)} %ens.1, f32[32,512]{1,0:T(8,128)} %innov.1, f32[2,512]{1,0:T(2,128)} %coords.1), custom_call_target="tpu_custom_call" | custom-call | tf_op jit(solution)/shard_map/update/pallas_call | solution.py:268
  113.7 2.0 %copy.8 = f32[1024,1024]{1,0:T(8,128)} copy(f32[1024,1024]{1,0:T(8,128)S(1)} %update.1) | data formatting | bytes 8388608

commit v3 on v2

--- a/solution.py
+++ b/solution.py
@@ -106,10 +106,13 @@
         cols = pl.ds(pl.multiple_of(to * PTS + k * BLK, BLK), BLK)
         remote(state.at[:, cols], xbuf.at[k, rows(me), :], a_send, a_recv.at[k], (d, to)).start()
 
-    def send_near(k, c):
-        for dz, dy in ((1, 0), (-1, 0), (0, 1), (0, -1)):
-            send_to(k, mem_of(dz, dy))
-        return c
+    def send(shifts, first, end):
+        def one(k, c):
+            for dz, dy in shifts:
+                send_to(k, mem_of(dz, dy))
+            return c
+
+        lax.fori_loop(first, end, one, 0)
 
     def send_state(k):
         def one(i, c):
@@ -132,26 +135,45 @@
         push(half(1, hi), hi, 0, -1, y_send)
         push_x(hi)
 
+    def pass_token(n, side):
+        for w in range(2):
+            signal(token.at[n, w], side[w])
+
+    def await_token(n):
+        for w in range(2):
+            pl.semaphore_wait(token.at[n, w], 1)
+
+    near_z, near_y = [(1, 0), (-1, 0)], [(0, 1), (0, -1)]
+    pass_token(0, around[2:])
     push_z(me, 1)
     push_z(me, -1)
+    send(near_z, 0, 2)
+    await_token(0)
+    pass_token(1, around[:2])
     push_y(me)
+    send(near_z, 2, NB - 1)
+    push_x(me)
     coord_copies = [
         remote(coords, crd.at[2], crd_send.at[0], crd_recv.at[1], (left, me)),
         remote(coords, crd.at[0], crd_send.at[1], crd_recv.at[0], (right, me)),
     ]
     for c in coord_copies:
         c.start()
-    lax.fori_loop(0, NB - 1, send_near, 0)
-    push_x(me)
+    send(near_y, 0, NB - 1)
+    await_token(1)
+    for n in range(1, ZN // 2 + 1):
+        if n < ZN // 2:
+            pass_token(n + 1, around[:2])
+        if n == 1:
+            send([(dz, dy) for dz in (1, -1) for dy in (2, 1, -1)], 0, 1)
+            send([(0, 2)], 0, 1)
+        else:
+            for dz in ([n, -n] if n < ZN // 2 else [n]):
+                send([(dz, dy) for dy in (2, 1, -1, 0)], 0, 1)
+        if n < ZN // 2:
+            await_token(n + 1)
     for k in range(NB):
         own_state(k).start()
-    for n in range(5):
-        side = around[:2] if n < 3 else around[2:]
-        for w in range(2):
-            signal(token.at[n, w], side[w])
-        for w in range(2):
-            pl.semaphore_wait(token.at[n, w], 1)
-    send_state(0)
     for s in range(1, ZN // 2 + 1):
         if s < ZN // 2:
             up, down = mem_of(-s, 0), mem_of(s, 0)
@@ -184,7 +206,7 @@
     lax.fori_loop(0, ZN, far, 0)
     send_state(6)
     send_state(7)
-    send_near(NB - 1, 0)
+    send(near_z + near_y, NB - 1, NB)
 
     def prepare(slot):
         def one(j, c):

time: 116 us -> 115 us (level)
  no operation moved by 1% of the time
where the time goes in v3:
time: 115 us
  Pallas kernels  112 us (97%)
  local copies, waits for them, and re-layouts  2.02 us (2%)
    pallas_call x1, Pallas kernels, shards(): pl.pallas_call(kernel, out_shape=pltpu.VMEM((M, PTS), f32), in_specs=[hbm...  112 us

profile of v3, /device:TPU:2, one launch (start us, length us, event | category | flops | bytes accessed | tf_op | source)
XLA Modules:
  0.0 115.1 jit_solution(9112685470208637139)
XLA Ops:
  0.7 112.5 %update.1 = f32[1024,1024]{1,0:T(8,128)S(1)} custom-call(s32[2,48]{1,0:T(2,128)} %bitcast.1, s32[1,1]{1,0:T(1,128)S(6)} %copy.9.count, f32[32,32768]{1,0:T(8,128)} %state.1, f32[32,512]{1,0:T(8,128)} %ens.1, f32[32,512]{1,0:T(8,128)} %innov.1, f32[2,512]{1,0:T(2,128)} %coords.1), custom_call_target="tpu_custom_call" | custom-call | tf_op jit(solution)/shard_map/update/pallas_call | solution.py:290
  113.1 2.0 %copy.8 = f32[1024,1024]{1,0:T(8,128)} copy(f32[1024,1024]{1,0:T(8,128)S(1)} %update.1) | data formatting | bytes 8388608

commit v4 on v3

--- a/solution.py
+++ b/solution.py
@@ -24,6 +24,47 @@
     return high, (v - high.astype(f32)).astype(bf16)
 
 
+def weights(x, ah, al, taper):
+    xh, xl = halves(x)
+    xs = jnp.concatenate([xh, xl], axis=1)
+    c1 = jnp.dot(ah, xs, preferred_element_type=f32)
+    c2 = jnp.dot(al, xh, preferred_element_type=f32)
+    wh, wl = halves(taper * (c1[:, :BLK] + (c1[:, BLK:] + c2)))
+    return wh, jnp.concatenate([wh, wl], axis=1)
+
+
+def moved(x, ih, il, wh, ws):
+    r1 = jnp.dot(ih, ws, preferred_element_type=f32)
+    r2 = jnp.dot(il, wh, preferred_element_type=f32)
+    return x + (r1[:, :BLK] + (r1[:, BLK:] + r2))
+
+
+def updated(x, ah, al, ih, il, taper):
+    return moved(x, ih, il, *weights(x, ah, al, taper))
+
+
+def finish(part, ah, al, ih, il, taper, out, piece, sem):
+    done = (NB - 1) * BLK
+    before = []
+    for n in range(4):
+        rows = pl.ds(n * (M // 4), M // 4)
+        before.append(
+            pltpu.make_async_copy(part.at[rows, pl.ds(0, done)], out.at[rows, pl.ds(0, done)], sem.at[n])
+        )
+    for c in before:
+        c.start()
+    wh, ws = weights(part[:, done:], ah[...], al[...], taper[...])
+    after = []
+    for n in range(4):
+        rows = pl.ds(n * (M // 4), M // 4)
+        piece[rows, :] = moved(part[rows, done:], ih[rows, :], il[rows, :], wh, ws)
+        c = pltpu.make_async_copy(piece.at[rows, :], out.at[rows, pl.ds(done, BLK)], sem.at[4 + n])
+        c.start()
+        after.append(c)
+    for c in before + after:
+        c.wait()
+
+
 def remote(src, dst, send, recv, device):
     return pltpu.make_async_remote_copy(
         src_ref=src,
@@ -36,7 +77,8 @@
 
 
 def kernel(
-    tiles_hbm, count, state, ens, innov, coords, out,
+    tiles_hbm, count, state, ens, innov, coords,
+    out, last_ah, last_al, last_ih, last_il, last_taper,
     tiles, xbuf, win, crd, at_hi, at_lo, in_hi, in_lo, cx, cy,
     obs_local, own_local, crd_send, z_send, y_send, x_send, a_send,
     blk_recv, x_recv, crd_recv, a_recv, token,
@@ -134,6 +176,22 @@
         take(hi)
         push(half(1, hi), hi, 0, -1, y_send)
         push_x(hi)
+
+    def ring(s):
+        if s < ZN // 2:
+            for m, way, t in ((mem_of(-s, 0), 1, 0), (mem_of(s, 0), -1, 1)):
+                take(m)
+                if s < ZN // 2 - 1:
+                    push_z(m, way)
+                else:
+                    push(half(t, m), m, way, 0, z_send)
+                push_y(m)
+                push_x(m)
+        else:
+            m = mem_of(s, 0)
+            take(m)
+            push_y(m)
+            push_x(m)
 
     def pass_token(n, side):
         for w in range(2):
@@ -165,6 +223,7 @@
         if n < ZN // 2:
             pass_token(n + 1, around[:2])
         if n == 1:
+            ring(1)
             send([(dz, dy) for dz in (1, -1) for dy in (2, 1, -1)], 0, 1)
             send([(0, 2)], 0, 1)
         else:
@@ -175,21 +234,8 @@
     for k in range(NB):
         own_state(k).start()
     for s in range(1, ZN // 2 + 1):
-        if s < ZN // 2:
-            up, down = mem_of(-s, 0), mem_of(s, 0)
-            for m, way, t in ((up, 1, 0), (down, -1, 1)):
-                take(m)
-                if s < ZN // 2 - 1:
-                    push_z(m, way)
-                else:
-                    push(half(t, m), m, way, 0, z_send)
-                push_y(m)
-                push_x(m)
-        else:
-            m = mem_of(s, 0)
-            take(m)
-            push_y(m)
-            push_x(m)
+        if s > 1:
+            ring(s)
         column(1 - s)
         if s > 1:
             column(s - 1)
@@ -231,19 +277,8 @@
         pltpu.make_async_copy(win.at[slot], win.at[slot], x_recv.at[n]).wait()
         prepare(slot)
 
-    def piece(k, c):
-        got = xbuf.at[k, pl.ds(0, M - ROWS), :]
-        pltpu.make_async_copy(got, got, a_recv.at[k]).wait()
-        own_state(k).wait()
+    def gather(k):
         ids = [tiles[1, k * TPB + t] for t in range(TPB)]
-        x = xbuf[k]
-        xh, xl = halves(x)
-        xs = jnp.concatenate([xh, xl], axis=1)
-        ah = jnp.concatenate([at_hi[b] for b in ids], axis=0)
-        al = jnp.concatenate([at_lo[b] for b in ids], axis=0)
-        c1 = jnp.dot(ah, xs, preferred_element_type=f32)
-        c2 = jnp.dot(al, xh, preferred_element_type=f32)
-        cov = c1[:, :BLK] + (c1[:, BLK:] + c2)
         lane = lax.broadcasted_iota(jnp.int32, (1, BLK), 1)
         px = d.astype(f32) + (lax.rem(lane, 32).astype(f32) + 0.5) / 32.0
         first = me * (PTS // 32) + k * (BLK // 32)
@@ -254,20 +289,31 @@
             gx = jnp.minimum(gx, float(DOM) - gx)
             gy = py - cy[ids[t]]
             taper = jnp.exp(-(gx * gx + gy * gy) / (2.0 * taper_reach * taper_reach))
-            alive = jnp.where(k * TPB + t < count[0, 0], 1.0 / (M - 1), 0.0)
-            w.append(taper * cov[t * BLK : (t + 1) * BLK] * alive)
-        wh, wl = halves(jnp.concatenate(w, axis=0))
-        ws = jnp.concatenate([wh, wl], axis=1)
-        ih = jnp.concatenate([in_hi[b] for b in ids], axis=1)
-        il = jnp.concatenate([in_lo[b] for b in ids], axis=1)
-        r1 = jnp.dot(ih, ws, preferred_element_type=f32)
-        r2 = jnp.dot(il, wh, preferred_element_type=f32)
-
+            w.append(taper * jnp.where(k * TPB + t < count[0, 0], 1.0 / (M - 1), 0.0))
+        return (
+            jnp.concatenate([at_hi[b] for b in ids], axis=0),
+            jnp.concatenate([at_lo[b] for b in ids], axis=0),
+            jnp.concatenate([in_hi[b] for b in ids], axis=1),
+            jnp.concatenate([in_lo[b] for b in ids], axis=1),
+            jnp.concatenate(w, axis=0),
+        )
+
+    def arrive(k):
+        got = xbuf.at[k, pl.ds(0, M - ROWS), :]
+        pltpu.make_async_copy(got, got, a_recv.at[k]).wait()
+        own_state(k).wait()
+
+    def piece(k, c):
+        arrive(k)
         cols = pl.ds(pl.multiple_of(k * BLK, BLK), BLK)
-        out[:, cols] = x + (r1[:, :BLK] + (r1[:, BLK:] + r2))
+        out[:, cols] = updated(xbuf[k], *gather(k))
         return c
 
-    lax.fori_loop(0, NB, piece, 0)
+    lax.fori_loop(0, NB - 1, piece, 0)
+    for ref, v in zip((last_ah, last_al, last_ih, last_il, last_taper), gather(NB - 1)):
+        ref[...] = v
+    arrive(NB - 1)
+    out[:, (NB - 1) * BLK :] = xbuf[NB - 1]
 
     def drain(ref, sem):
         pltpu.make_async_copy(ref, ref, sem).wait()
@@ -287,11 +333,19 @@
     hbm = pl.BlockSpec(memory_space=pltpu.HBM)
     vmem = pl.BlockSpec(memory_space=pltpu.VMEM)
     dma = pltpu.SemaphoreType.DMA
-    return pl.pallas_call(
+    kept = (
+        pltpu.VMEM((M, PTS), f32),
+        pltpu.VMEM((TPB * BLK, M), bf16),
+        pltpu.VMEM((TPB * BLK, M), bf16),
+        pltpu.VMEM((M, TPB * BLK), bf16),
+        pltpu.VMEM((M, TPB * BLK), bf16),
+        pltpu.VMEM((TPB * BLK, BLK), f32),
+    )
+    held = pl.pallas_call(
         kernel,
-        out_shape=pltpu.VMEM((M, PTS), f32),
+        out_shape=kept,
         in_specs=[hbm, pl.BlockSpec(memory_space=pltpu.SMEM), hbm, hbm, hbm, hbm],
-        out_specs=vmem,
+        out_specs=(vmem,) * 6,
         scratch_shapes=[
             pltpu.SMEM((2, TPB * NB), jnp.int32),
             pltpu.VMEM((NB, M, BLK), f32),
@@ -317,10 +371,19 @@
             pltpu.SemaphoreType.REGULAR((5, 2)),
         ],
         compiler_params=pltpu.CompilerParams(
-            collective_id=0, has_side_effects=True, vmem_limit_bytes=48 * 1024 * 1024
+            collective_id=0, has_side_effects=True, vmem_limit_bytes=46 * 1024 * 1024
         ),
         name="update",
     )(*(pinned(a) for a in (tile_list[0, 0], tile_counts, state, obs_ensemble, innovations, obs_coords)))
+    return pl.pallas_call(
+        finish,
+        out_shape=jax.ShapeDtypeStruct((M, PTS), f32),
+        in_specs=[vmem] * 6,
+        out_specs=pl.BlockSpec(memory_space=pl.ANY),
+        scratch_shapes=[pltpu.VMEM((M, BLK), f32), dma((8,))],
+        compiler_params=pltpu.CompilerParams(vmem_limit_bytes=16 * 1024 * 1024),
+        name="finish",
+    )(*(pltpu.with_memory_space_constraint(a, pltpu.VMEM) for a in held))
 
 
 def solution(mesh):

time: 115 us -> 114 us (level)
  local copies, waits for them, and re-layouts: 2.02 us -> 0 us
    unnamed x1 -> x0, local copies, waits for them, and re-layouts: 2.02 us -> none
    pallas_call x1 -> x2, Pallas kernels: 112 us -> 113 us  [the longest x1 110 us: shards(): pl.pallas_call(kernel, out_shape=kept, in_specs=[hbm, pl.BlockSpec(memory...]
where the time goes in v4:
time: 114 us
  Pallas kernels  113 us (99%)
    pallas_call x1, Pallas kernels, shards(): pl.pallas_call(kernel, out_shape=kept, in_specs=[hbm, pl.BlockSpec(memory...  110 us
    pallas_call x1, Pallas kernels, shards(): pl.pallas_call(finish, out_shape=jax.ShapeDtypeStruct((M, PTS), f32), in_...  2.61 us

profile of v4, /device:TPU:2, one launch (start us, length us, event | category | flops | bytes accessed | tf_op | source)
XLA Modules:
  0.0 113.6 jit_solution(16361764212638024480)
XLA Ops:
  0.7 110.4 %update.1 = (f32[1024,1024]{1,0:T(8,128)S(1)}, bf16[768,1024]{1,0:T(8,128)(2,1)S(1)}, bf16[768,1024]{1,0:T(8,128)(2,1)S(1)}, bf16[1024,768]{1,0:T(8,128)(2,1)S(1...) custom-call(s32[2,48]{1,0:T(2,128)} %bitcast.1, s32[1,1]{1,0:T(1,128)S(6)} %copy.7.count, f32[32,32768]{1,0:T(8,128)} %state.1, ...), custom_call_target="tpu_custom_call" | custom-call | tf_op jit(solution)/shard_map/update/pallas_call | solution.py:344
  111.0 2.6 %finish.1 = f32[1024,1024]{1,0:T(8,128)} custom-call(f32[1024,1024]{1,0:T(8,128)S(1)} %get-tuple-element.11.part, bf16[768,1024]{1,0:T(8,128)(2,1)S(1)} %get-tuple-element.12.ah, bf16[768,1024]{1,0:T(8,128)(2,1)S(1)} %get-tuple-element.13.al, bf16[1024,768]{1,0:T(8,128)(2,1)S(1)} %get-tuple-element.14.ih, bf16[1024,768]{1,0:T(8,128)(2,1)S(1)} %get-tuple-element.15.il, ...), custom_call_target="tpu_custom_call" | custom-call | tf_op jit(solution)/shard_map/finish/pallas_call | solution.py:378
